TPU v7x, 256 devices: a whole 4x4x8 slice. The times are simulated.
256 devices in a mesh: dp: 32 (over x_hi, z, core), tensor: 8 (over y, x_lo).
Axes of the slice: x: 4 (x_hi: 2, x_lo: 2; x = x_hi * 2 + x_lo), y: 4, z: 8, core: 2. Of those that a mesh axis runs over, the one named last changes fastest.
Arguments:
- master: float32 [2, 16384, 16384], P(None, ('tensor', 'dp')), may hold values from -0.1875 to 0.1875
- tile_order: int32 [8, 16], P('tensor'), may hold values from 0 to 15, each once within a row
- check_weights: int32 [8, 16384], P(None, 'tensor'), may hold values from -7 to 7
Outputs:
- tiled: bfloat16 [2, 16384, 16384], P(None, 'tensor', 'dp')
- checksum: float32 [2, 8, 16384], P(None, None, ('dp', 'tensor'))
Inputs may be any that keep to these rules, and one draw needn't show every extreme that they name: Each row of tile_order lists every number of 0 to 15 once.
All inputs are finite; a program needn't handle non-finite values.
Results may differ from a plain program's by a relative error of at most 0.0029.
Values may be sent and summed in bfloat16 or wider, within the bound.
No kernel may reach another device: no remote copies, remote signals or barrier semaphores. Data moves between devices by JAX's collectives and lax.ppermute only.
A program may use at most 128 MiB of HBM per device.

v0:
```python
import jax
import jax.numpy as jnp
from jax import lax
from jax.sharding import PartitionSpec as P

TILE = 128


def on_device(master, tile_order, check_weights):
    tile_rows = TILE
    order = tile_order[0]
    count = order.shape[0]
    low = master.astype(jnp.bfloat16)
    weights = check_weights.astype(jnp.bfloat16)
    received = lax.all_to_all(low, "dp", split_axis=2, concat_axis=1, tiled=True)
    items = received.shape[0]
    columns = received.shape[2]
    blocks = received.reshape(items, count, tile_rows, columns)
    moved = jnp.take(blocks, order, axis=1)
    tiled = moved.reshape(items, count * tile_rows, columns)
    partial_sums = jnp.einsum("cr,lrd->lcd", weights, tiled, preferred_element_type=jnp.float32)
    checksum = lax.psum_scatter(partial_sums, "tensor", scatter_dimension=2, tiled=True)
    return (tiled, checksum)


def solution(mesh):
    in_specs = (P(None, ("tensor", "dp"), None), P("tensor", None), P(None, "tensor"))
    out_specs = (P(None, "tensor", "dp"), P(None, None, ("dp", "tensor")))
    return jax.shard_map(
        on_device, mesh=mesh, in_specs=in_specs, out_specs=out_specs, check_vma=False
    )
```

profile of v0, /device:TPU:4, one launch (start us, length us, event | category | flops | bytes accessed | tf_op | source)
XLA Modules:
  0.0 244.3 jit_solution(6594867219500252485)
XLA Ops:
  7.2 5.9 %convert_element_type.6 = bf16[2,64,16384]{2,1,0:T(8,128)(2,1)} convert(f32[2,64,16384]{2,1,0:T(8,128)} %param.3) | non-fusion elementwise | flops 2097152 | bytes 12582912 | tf_op jit(solution)/shard_map/convert_element_type | solution.py:13
  13.1 17.8 %copy.7 = bf16[2,64,16384]{1,0,2:T(2,128)(2,1)} copy(bf16[2,64,16384]{2,1,0:T(8,128)(2,1)} %convert_element_type.6) | data formatting | bytes 8388608 | tf_op jit(solution)/shard_map/convert_element_type | solution.py:13
  30.9 13.9 %reshape.57 = bf16[32,2,32768]{2,1,0:T(2,128)(2,1)} reshape(bf16[16384,2,64]{2,1,0:T(2,128)(2,1)} %bitcast.26) | data formatting | bytes 8388608
  44.7 0.0 copy-start.2
  44.7 11.8 %all-to-all-start = ((bf16[32,2,32768]{2,1,0:T(2,128)(2,1)}), bf16[32,2,32768]{2,1,0:T(2,128)(2,1)}, u32[]{:S(2)}, u32[]{:S(2)}) async-start(bf16[32,2,32768]{2,1,0:T(2,128)(2,1)} %reshape.57), calls=%async_computation | async-start | bytes 8388608 | tf_op jit(solution)/shard_map/all_to_all | solution.py:15
  56.5 0.0 reduce-scatter.4.cloned.1.call-start
  56.6 0.0 copy-done.2
  56.6 0.1 broadcast_bitcast_fusion
  56.7 93.7 %all-to-all-done = bf16[32,2,32768]{2,1,0:T(2,128)(2,1)} async-done(((bf16[32,2,32768]{2,1,0:T(2,128)(2,1)}), bf16[32,2,32768]{2,1,0:T(2,128)(2,1)}, u32[]{:S(2)}, u32[]{:S(2)}) %all-to-all-start) | async-done | bytes 4194336 | tf_op jit(solution)/shard_map/all_to_all | solution.py:15
  150.3 13.7 %reshape.58 = bf16[16384,2,64]{2,1,0:T(2,128)(2,1)} reshape(bf16[32,2,32768]{2,1,0:T(2,128)(2,1)} %all-to-all-done) | data formatting | bytes 8388608
  164.0 18.5 %copy.12 = bf16[2,64,32,512]{3,1,2,0:T(8,128)(2,1)} copy(bf16[2,64,32,512]{1,0,3,2:T(2,128)(2,1)} %bitcast.27) | data formatting | bytes 8388608 | tf_op jit(solution)/shard_map/all_to_all | solution.py:15
  182.5 4.9 %gather_fusion = bf16[16,2,128,512]{3,2,1,0:T(8,128)(2,1)} fusion(bf16[2,16,128,512]{3,2,1,0:T(8,128)(2,1)} %bitcast.28, s32[1024]{0:T(1024)S(1)} %pad_clamp_fusion), kind=kCustom, calls=%fused_computation | custom fusion | bytes 8388672 | tf_op jit(solution)/shard_map/jit(_take)/gather | solution.py:19
  187.5 2.6 %copy.10 = bf16[2,16,128,512]{3,2,1,0:T(8,128)(2,1)S(1)} copy(bf16[2,16,128,512]{3,2,0,1:T(8,128)(2,1)} %bitcast.29) | data formatting | bytes 8388608 | tf_op jit(solution)/shard_map/jit(_take)/gather | solution.py:19
  190.1 0.0 copy-start.1
  190.1 0.9 bitcast_select_fusion
  191.0 0.0 copy-start
  191.0 2.0 copy-done
  193.0 0.0 copy-done.1
  193.0 0.6 convolution_bitcast_fusion
  193.7 0.3 copy.13
  193.9 1.0 reshape.55
  194.9 0.0 reduce-scatter.4.cloned.1.call-update
  194.9 41.0 %reduce-scatter.4.cloned.1.call-done = f32[64,16]{1,0:T(8,128)} async-done(((f32[512,16]{1,0:T(8,128)}), f32[64,16]{1,0:T(8,128)}) %reduce-scatter.4.cloned.1.call-update) | async-done | bytes 4112
  235.9 0.9 reshape.56
  236.8 0.7 copy.14
  (3 shorter events, 0.0 us)
Async XLA Ops:
  44.7 11.8 %copy-start.2 = (s32[1,16]{1,0:T(1,128)S(1)}, s32[1,16]{1,0:T(1,128)}, u32[]{:S(2)}) copy-start(s32[1,16]{1,0:T(1,128)} %param.4) | copy-start | bytes 196
  44.7 105.6 %all-to-all-start = ((bf16[32,2,32768]{2,1,0:T(2,128)(2,1)}), bf16[32,2,32768]{2,1,0:T(2,128)(2,1)}, u32[]{:S(2)}, u32[]{:S(2)}) async-start(bf16[32,2,32768]{2,1,0:T(2,128)(2,1)} %reshape.57), calls=%async_computation | async-start | bytes 8388608 | tf_op jit(solution)/shard_map/all_to_all | solution.py:15
  56.5 179.4 %reduce-scatter.4.cloned.1.call-start = ((), (), s32[]{:S(2)}) async-start(), calls=%async_computation.2 | async-start | bytes 294912
  190.1 2.9 %copy-start.1 = (s32[8,2048]{1,0:T(8,128)S(1)}, s32[8,2048]{1,0:T(8,128)}, u32[]{:S(2)}) copy-start(s32[8,2048]{1,0:T(8,128)} %param.5) | copy-start | bytes 196612
  191.0 2.0 copy-start
Sparse Core Ops, SparseCore 0:
  195.1 40.8 reduce-scatter.3
where the time goes:
time: 246 us; the launch traced here: 244 us
  waiting for transfers between devices  135 us (55%)
  local copies, waits for them, and re-layouts  76.3 us (31%)
  between operations  14.1 us (6%)
  starting transfers between devices  11.8 us (5%)
  other arithmetic  6.79 us (3%)
    all_to_all x1, waiting for transfers between devices, on_device(): lax.all_to_all(low, 'dp', split_axis=2, concat_axis=1, tiled=True)  93.7 us
    unnamed x2, waiting for transfers between devices  41 us
    unnamed x12, local copies, waits for them, and re-layouts  32.3 us
    all_to_all x1, local copies, waits for them, and re-layouts, on_device(): lax.all_to_all(low, 'dp', split_axis=2, concat_axis=1, tiled=True)  18.5 us
    convert_element_type x1, local copies, waits for them, and re-layouts, on_device(): low = master.astype(jnp.bfloat16)  17.8 us
    all_to_all x1, starting transfers between devices, on_device(): lax.all_to_all(low, 'dp', split_axis=2, concat_axis=1, tiled=True)  11.8 us
    gather x2, local copies, waits for them, and re-layouts, on_device(): moved = jnp.take(blocks, order, axis=1)  7.57 us
    convert_element_type x1, other arithmetic, on_device(): low = master.astype(jnp.bfloat16)  5.9 us
  transfers between devices with their start and end apart: 2, of which 2 were waited for; matrix products, arithmetic and copies ran while one was open for 0% of the time, Pallas kernels for 0%

commit v1 on v0

--- a/solution.py
+++ b/solution.py
@@ -12,7 +12,9 @@
     count = order.shape[0]
     low = master.astype(jnp.bfloat16)
     weights = check_weights.astype(jnp.bfloat16)
-    received = lax.all_to_all(low, "dp", split_axis=2, concat_axis=1, tiled=True)
+    received = jnp.concatenate(
+        lax.all_to_all(jnp.stack(jnp.split(low, lax.axis_size("dp"), axis=2)), "dp", 0, 0), axis=1
+    )
     items = received.shape[0]
     columns = received.shape[2]
     blocks = received.reshape(items, count, tile_rows, columns)

time: 246 us -> 205 us (0.83)
  local copies, waits for them, and re-layouts: 76.3 us -> 38.4 us
    convert_element_type x1 -> x0, local copies, waits for them, and re-layouts: 17.8 us -> none  [on_device(): low = master.astype(jnp.bfloat16)]
    all_to_all x1, local copies, waits for them, and re-layouts: 18.5 us -> 4.7 us  [on_device(): lax.all_to_all(jnp.stack(jnp.split(low, lax.axis_size('dp'), axis=2)), 'd...]
    unnamed x12 -> x41, local copies, waits for them, and re-layouts: 32.3 us -> 25.4 us
where the time goes in v1:
time: 205 us; the launch traced here: 204 us
  waiting for transfers between devices  135 us (66%)
  local copies, waits for them, and re-layouts  38.4 us (19%)
  between operations  14.1 us (7%)
  starting transfers between devices  11.8 us (6%)
  other arithmetic  4.76 us (2%)
    all_to_all x1, waiting for transfers between devices, on_device(): lax.all_to_all(jnp.stack(jnp.split(low, lax.axis_size('dp'), axis=2)), 'd...  93.7 us
    unnamed x2, waiting for transfers between devices  41 us
    unnamed x41, local copies, waits for them, and re-layouts  25.4 us
    all_to_all x1, starting transfers between devices, on_device(): lax.all_to_all(jnp.stack(jnp.split(low, lax.axis_size('dp'), axis=2)), 'd...  11.8 us
    gather x2, local copies, waits for them, and re-layouts, on_device(): moved = jnp.take(blocks, order, axis=1)  7.57 us
    all_to_all x1, local copies, waits for them, and re-layouts, on_device(): lax.all_to_all(jnp.stack(jnp.split(low, lax.axis_size('dp'), axis=2)), 'd...  4.7 us
  transfers between devices with their start and end apart: 2, of which 2 were waited for; matrix products, arithmetic and copies ran while one was open for 0% of the time, Pallas kernels for 0%

profile of v1, /device:TPU:4, one launch (start us, length us, event | category | flops | bytes accessed | tf_op | source)
XLA Modules:
  0.0 204.4 jit_solution(17297433592261791428)
XLA Ops:
  7.2 3.9 %convert_element_type.6 = bf16[2,64,16384]{2,1,0:T(8,128)(2,1)S(1)} convert(f32[2,64,16384]{2,1,0:T(8,128)} %param.3) | non-fusion elementwise | flops 2097152 | bytes 12582912 | tf_op jit(solution)/shard_map/convert_element_type | solution.py:13
  11.0 0.7 fusion.31
  11.7 0.7 fusion.30
  12.4 0.7 fusion.29
  13.0 0.7 fusion.28
  13.7 0.7 fusion.27
  14.4 0.7 fusion.26
  15.0 0.7 fusion.25
  15.7 0.7 fusion.24
  16.4 0.7 fusion.23
  17.0 0.7 fusion.22
  17.7 0.7 fusion.21
  18.3 0.7 fusion.20
  19.0 0.7 fusion.19
  19.7 0.7 fusion.18
  20.3 0.7 fusion.17
  21.0 0.7 fusion.16
  21.7 0.7 fusion.15
  22.3 0.7 fusion.14
  23.0 0.7 fusion.13
  23.7 0.7 fusion.12
  24.3 0.7 fusion.11
  25.0 0.7 fusion.10
  25.7 0.7 fusion.9
  26.3 0.7 fusion.8
  27.0 0.7 fusion.7
  27.6 0.7 fusion.6
  28.3 0.7 fusion.5
  29.0 0.7 fusion.4
  29.6 0.7 fusion.3
  30.3 0.7 fusion.2
  31.0 0.7 fusion.1
  31.6 0.7 fusion
  32.3 11.8 %all-to-all-start = ((bf16[32,2,64,512]{3,2,1,0:T(8,128)(2,1)}), bf16[32,2,64,512]{3,2,1,0:T(8,128)(2,1)}, u32[]{:S(2)}, u32[]{:S(2)}) async-start(bf16[32,2,64,512]{3,2,1,0:T(8,128)(2,1)} %fusion), calls=%async_computation | async-start | bytes 8388608 | tf_op jit(solution)/shard_map/all_to_all | solution.py:16
  44.1 0.0 reduce-scatter.4.cloned.1.call-start
  44.2 0.1 broadcast_bitcast_fusion
  44.3 93.7 %all-to-all-done = bf16[32,2,64,512]{3,2,1,0:T(8,128)(2,1)} async-done(((bf16[32,2,64,512]{3,2,1,0:T(8,128)(2,1)}), bf16[32,2,64,512]{3,2,1,0:T(8,128)(2,1)}, u32[]{:S(2)}, u32[]{:S(2)}) %all-to-all-start) | async-done | bytes 4194336 | tf_op jit(solution)/shard_map/all_to_all | solution.py:16
  137.9 4.7 %copy.68 = bf16[32,2,64,512]{3,2,0,1:T(8,128)(2,1)} copy(bf16[32,2,64,512]{3,2,1,0:T(8,128)(2,1)} %all-to-all-done) | data formatting | bytes 8388608 | tf_op jit(solution)/shard_map/all_to_all | solution.py:16
  142.6 4.9 %gather_fusion = bf16[16,2,128,512]{3,2,1,0:T(8,128)(2,1)} fusion(bf16[2,16,128,512]{3,2,1,0:T(8,128)(2,1)} %bitcast.150, s32[1024]{0:T(1024)S(1)} %pad_clamp_fusion), kind=kCustom, calls=%fused_computation | custom fusion | bytes 8388672 | tf_op jit(solution)/shard_map/jit(_take)/gather | solution.py:21
  147.6 2.6 %copy.69 = bf16[2,16,128,512]{3,2,1,0:T(8,128)(2,1)S(1)} copy(bf16[2,16,128,512]{3,2,0,1:T(8,128)(2,1)} %bitcast.151) | data formatting | bytes 8388608 | tf_op jit(solution)/shard_map/jit(_take)/gather | solution.py:21
  150.2 0.9 bitcast_select_fusion
  151.1 2.0 copy-done
  153.1 0.6 convolution_bitcast_fusion
  153.7 0.3 copy.70
  154.0 1.0 reshape.54
  155.0 41.0 %reduce-scatter.4.cloned.1.call-done = f32[64,16]{1,0:T(8,128)} async-done(((f32[512,16]{1,0:T(8,128)}), f32[64,16]{1,0:T(8,128)}) %reduce-scatter.4.cloned.1.call-update) | async-done | bytes 4112
  196.0 0.9 reshape.55
  196.9 0.7 copy.71
  (9 shorter events, 0.0 us)
Async XLA Ops:
  32.3 11.8 %copy-start.2 = (s32[1,16]{1,0:T(1,128)S(1)}, s32[1,16]{1,0:T(1,128)}, u32[]{:S(2)}) copy-start(s32[1,16]{1,0:T(1,128)} %param.4) | copy-start | bytes 196
  32.3 105.6 %all-to-all-start = ((bf16[32,2,64,512]{3,2,1,0:T(8,128)(2,1)}), bf16[32,2,64,512]{3,2,1,0:T(8,128)(2,1)}, u32[]{:S(2)}, u32[]{:S(2)}) async-start(bf16[32,2,64,512]{3,2,1,0:T(8,128)(2,1)} %fusion), calls=%async_computation | async-start | bytes 8388608 | tf_op jit(solution)/shard_map/all_to_all | solution.py:16
  44.1 151.9 %reduce-scatter.4.cloned.1.call-start = ((), (), s32[]{:S(2)}) async-start(), calls=%async_computation.2 | async-start | bytes 294912
  150.2 2.9 %copy-start.1 = (s32[8,2048]{1,0:T(8,128)S(1)}, s32[8,2048]{1,0:T(8,128)}, u32[]{:S(2)}) copy-start(s32[8,2048]{1,0:T(8,128)} %param.5) | copy-start | bytes 196612
  151.1 2.0 copy-start
Sparse Core Ops, SparseCore 0:
  155.2 40.8 reduce-scatter.3
